TPU v7x, 32 devices: a whole 2x2x4 slice. The times are simulated.
32 devices in a mesh: grp: 4 (over x, core), dev: 8 (over z, y).
Axes of the slice: x: 2, y: 2, z: 4, core: 2. Of those that a mesh axis runs over, the one named last changes fastest.
Arguments:
- positions: float32 [3, 32768], P(None, ('grp', 'dev')), may hold values from -6 to 6
- rotations: float32 [9, 32768], P(None, ('grp', 'dev')), may hold values from -1 to 1, as said below
- clump_kind: int32 [32768], P(('grp', 'dev')), may hold values from 0 to 7
- sub_offsets: int32 [8, 3, 64], replicated, may hold values from -8 to 8
- pair_blocks: int32 [2, 32768], P(None, ('grp', 'dev')), may hold values from 0 to 16383, as said below
- pair_count: int32 [32], P(('grp', 'dev')), may hold values from 1 to 1024, as said below
Outputs:
- clump_force: float32 [3, 32768], P(None, ('grp', 'dev'))
- clump_torque: float32 [3, 32768], P(None, ('grp', 'dev'))
Inputs may be any that keep to these rules, and one draw needn't show every extreme that they name: `rotations`: each column is a proper rotation matrix in row-major order. `pair_blocks`: the two blocks of a slot differ. A slot on a device of group g names as its first block one of group g's blocks (g * 4096 to (g + 1) * 4096 - 1) and as its second one of group g's blocks or of the 128 nearest blocks of groups g - 1 and g + 1, that is a block from g * 4096 - 128 to (g + 1) * 4096 + 127. `pair_count`: each device has at least one live slot.
All inputs are finite; a program needn't handle non-finite values.
Results may differ from a plain program's by a relative error of at most 0.0003.
Values sent between devices are 32-bit elements; how exact they have to be, the bound alone decides.
No kernel may reach another device: no remote copies, remote signals or barrier semaphores. Data moves between devices by JAX's collectives and lax.ppermute only.
A program may use at most 128 MiB of HBM per device.

v0:
```python
import jax
import jax.numpy as jnp
from jax import lax
from jax.sharding import PartitionSpec as P

RIM = 128


OFFSET_UNIT = 0.125
REACH_SQUARED = 4.0
STIFFNESS = 1.0 / 256.0


def padded(cells, sides, width):
    for axis, dim in sides:
        count = lax.axis_size(axis)
        ends = count - 1
        head = lax.slice_in_dim(cells, 0, width, axis=dim)
        tail = lax.slice_in_dim(cells, cells.shape[dim] - width, cells.shape[dim], axis=dim)
        cells = jnp.concatenate(
            [
                lax.ppermute(tail, axis, [(i, (i + 1) % count) for i in range(ends)]),
                cells,
                lax.ppermute(head, axis, [((i + 1) % count, i) for i in range(ends)]),
            ],
            axis=dim,
        )
    return cells


def cross_axis(left_vec, right_vec):
    return jnp.stack(
        [
            left_vec[1] * right_vec[2] - left_vec[2] * right_vec[1],
            left_vec[2] * right_vec[0] - left_vec[0] * right_vec[2],
            left_vec[0] * right_vec[1] - left_vec[1] * right_vec[0],
        ],
        0,
    )


def place_blocks(centers, rotation_rows, onehot, offset_table):
    sub_count = offset_table.shape[1] // 3
    offsets = jnp.dot(onehot, offset_table, precision=lax.Precision.HIGHEST).reshape(
        -1, 3, sub_count
    )
    rotation_mats = rotation_rows.T.reshape(-1, 3, 3)
    world_pos = centers.T[:, :, None] + jnp.einsum(
        "ckm,cms->cks", rotation_mats, offsets, precision=lax.Precision.HIGHEST
    )
    block_count = world_pos.shape[0] // 2
    return (
        world_pos.reshape(block_count, 2, 3, sub_count)
        .transpose(0, 2, 1, 3)
        .reshape(block_count, 3, 2 * sub_count)
    )


def contact(near_pos, far_pos):
    separation = near_pos[:, :, None] - far_pos[:, None, :]
    squared = jnp.sum(separation * separation, 0)
    weights = STIFFNESS * jnp.maximum(REACH_SQUARED - squared, 0.0)
    pushes = weights[None] * separation
    return (jnp.sum(pushes, 2), -jnp.sum(pushes, 1))


def anchor_moments(sphere_block, force_block):
    sub_count = sphere_block.shape[1] // 2
    spots = sphere_block.reshape(3, 2, sub_count)
    pushes = force_block.reshape(3, 2, sub_count)
    return jnp.concatenate([jnp.sum(pushes, -1), jnp.sum(cross_axis(spots, pushes), -1)], 0)


def shards(positions, rotations, clump_kind, sub_offsets, pair_blocks, pair_count):
    members = lax.axis_size("dev")
    group_index = lax.axis_index("grp")
    own_blocks = positions.shape[1] // 2
    group_blocks = own_blocks * members
    kind_count = sub_offsets.shape[0]
    sub_count = sub_offsets.shape[2]
    slot_group = 32
    offset_table = sub_offsets.astype(jnp.float32).reshape(kind_count, 3 * sub_count) * OFFSET_UNIT
    onehot = (clump_kind[:, None] == jnp.arange(kind_count, dtype=jnp.int32)[None, :]).astype(
        jnp.float32
    )
    own_spheres = place_blocks(positions, rotations, onehot, offset_table)
    gathered = lax.all_gather(own_spheres, "dev", axis=0, tiled=True)
    spheres = padded(gathered, (("grp", 0),), RIM)
    table_base = group_index * group_blocks - RIM
    first_local = pair_blocks[0] - table_base
    second_local = pair_blocks[1] - table_base
    live_count = pair_count[0]
    turn_count = (live_count + slot_group - 1) // slot_group
    table_rows = spheres.shape[0]
    zero_table = jnp.zeros((table_rows, 6, 2), jnp.float32)

    def visit_block(turn_index, totals):
        start_row = turn_index * slot_group
        first_block = lax.dynamic_slice_in_dim(first_local, start_row, slot_group, 0)
        second_block = lax.dynamic_slice_in_dim(second_local, start_row, slot_group, 0)
        live_part = (start_row + jnp.arange(slot_group, dtype=jnp.int32) < live_count).astype(
            jnp.float32
        )
        near_pos = spheres[first_block]
        far_pos = spheres[second_block]
        push_first, push_second = jax.vmap(contact)(near_pos, far_pos)
        weight_live = live_part[:, None, None]
        totals = totals.at[first_block].add(
            jax.vmap(anchor_moments)(near_pos, push_first) * weight_live
        )
        totals = totals.at[second_block].add(
            jax.vmap(anchor_moments)(far_pos, push_second) * weight_live
        )
        return totals

    totals = lax.fori_loop(0, turn_count, visit_block, zero_table)
    moments = totals.transpose(1, 0, 2).reshape(6, 2 * table_rows)
    rim_clumps = 2 * RIM
    rim_parts = jnp.concatenate(
        [moments[:, :rim_clumps], moments[:, moments.shape[1] - rim_clumps :]], 1
    )
    arrived = padded(rim_parts, (("grp", 1),), rim_clumps)
    interior = moments[:, rim_clumps : rim_clumps + 2 * group_blocks]
    interior = interior.at[:, :rim_clumps].add(arrived[:, :rim_clumps])
    interior = interior.at[:, interior.shape[1] - rim_clumps :].add(
        arrived[:, arrived.shape[1] - rim_clumps :]
    )
    summed = lax.psum_scatter(interior, "dev", scatter_dimension=1, tiled=True)
    clump_force = summed[0:3]
    clump_torque = summed[3:6] - cross_axis(positions, clump_force)
    return (clump_force, clump_torque)


def solution(mesh):
    placed = (
        P(None, ("grp", "dev")),
        P(None, ("grp", "dev")),
        P(("grp", "dev")),
        P(),
        P(None, ("grp", "dev")),
        P(("grp", "dev")),
    )
    return jax.shard_map(
        shards,
        mesh=mesh,
        in_specs=placed,
        out_specs=(P(None, ("grp", "dev")), P(None, ("grp", "dev"))),
        check_vma=False,
    )
```

profile of v0, /device:TPU:0, one launch (start us, length us, event | category | flops | bytes accessed | tf_op | source)
XLA Modules:
  0.0 1036.6 jit_solution(15804710355770445196)
XLA Ops:
  13.1 9.8 convolution_add_fusion
  26.1 100.9 %all-gather.2.cloned.1.call-done = f32[4096,3,128]{0,2,1:T(8,128)} async-done(((f32[512,3,128]{0,2,1:T(8,128)}), f32[4096,3,128]{0,2,1:T(8,128)}) %all-gather.2.cloned.1.call-update) | async-done | bytes 6291472 | tf_op jit(solution)/shard_map/all_gather | solution.py:87
  130.7 3.7 collective-permute-done.1
  134.4 6.1 pad_maximum_fusion
  140.5 10.1 copy.151
  150.7 3.6 broadcast_in_dim.6
  154.3 297.2 %while.12 = (s32[]{:T(128)}, f32[4352,6,2]{1,2,0:T(2,128)}, s32[]{:T(128)}, s32[1024]{0:T(1024)S(1)}, f32[4352,3,128]{2,1,0:T(4,128)}, /*index=5*/s32[1024]{0:T(...) while((s32[]{:T(128)}, f32[4352,6,2]{1,2,0:T(2,128)}, ...), condition=%wide.region_10.11_spmd, body=%wide.region_0.10_spmd.sunk | while | flops 12222438 | bytes 10249395 | solution.py:116
  154.3 4.1 gather_fusion
  158.5 4.1 gather_fusion.1
  165.1 4.1 fusion.19
  171.7 3.6 scatter_fusion
  179.1 4.1 gather_fusion
  183.2 4.1 gather_fusion.1
  189.8 4.1 fusion.19
  196.4 3.6 scatter_fusion
  203.8 4.1 gather_fusion
  207.9 4.1 gather_fusion.1
  214.5 4.1 fusion.19
  221.2 3.6 scatter_fusion
  224.9 3.6 scatter_fusion.1
  228.6 4.1 gather_fusion
  232.7 4.1 gather_fusion.1
  239.3 4.1 fusion.19
  246.0 3.7 scatter_fusion
  249.7 3.6 scatter_fusion.1
  253.4 4.1 gather_fusion
  257.6 4.1 gather_fusion.1
  264.1 4.1 fusion.19
  274.5 3.6 scatter_fusion.1
  278.2 4.1 gather_fusion
  282.3 4.1 gather_fusion.1
  288.9 4.1 fusion.19
  295.5 3.6 scatter_fusion
  299.2 3.6 scatter_fusion.1
  302.9 4.1 gather_fusion
  307.1 4.1 gather_fusion.1
  313.7 4.1 fusion.19
  320.3 3.6 scatter_fusion
  327.6 4.1 gather_fusion
  331.8 4.1 gather_fusion.1
  338.4 4.1 fusion.19
  345.0 3.6 scatter_fusion
  348.7 3.7 scatter_fusion.1
  352.4 4.1 gather_fusion
  356.6 4.1 gather_fusion.1
  363.2 4.1 fusion.19
  369.8 3.6 scatter_fusion
  373.5 3.6 scatter_fusion.1
  377.2 4.1 gather_fusion
  381.4 4.1 gather_fusion.1
  388.0 4.1 fusion.19
  394.6 3.7 scatter_fusion
  398.4 3.6 scatter_fusion.1
  402.1 4.1 gather_fusion
  406.2 4.1 gather_fusion.1
  412.8 4.1 fusion.19
  423.1 3.6 scatter_fusion.1
  426.8 4.1 gather_fusion
  431.0 4.1 gather_fusion.1
  437.5 4.1 fusion.19
  444.2 3.6 scatter_fusion
  454.5 4.4 slice.176
  463.9 104.6 %collective-permute-done.3 = f32[6,256]{1,0:T(8,128)S(1)} collective-permute-done((f32[6,256]{1,0:T(8,128)S(1)}, f32[6,256]{1,0:T(8,128)S(1)}, u32[]{:S(2)}, u32[]{:S(2)}) %collective-permute-start.3) | collective-permute-done | bytes 6176 | tf_op jit(solution)/shard_map/ppermute | solution.py:24
  569.2 458.2 %reduce-scatter.2.cloned.1.call-done = f32[6,1024]{1,0:T(8,128)} async-done(((f32[6,8192]{1,0:T(8,128)}), f32[6,1024]{1,0:T(8,128)}) %reduce-scatter.2.cloned.1.call-update) | async-done | bytes 24592 | tf_op jit(solution)/shard_map/reduce_scatter | solution.py:128
  (380 shorter events, 105.1 us)
Async XLA Ops:
  7.2 5.7 copy-start.1
  7.2 119.8 %all-gather.2.cloned.1.call-start = ((), (), s32[]{:S(2)}) async-start(), calls=%async_computation.1 | async-start | bytes 7077888 | tf_op jit(solution)/shard_map/all_gather | solution.py:87
  13.1 117.6 %copy-start.2 = (s32[2,1024]{1,0:T(2,128)S(1)}, s32[2,1024]{1,0:T(2,128)}, u32[]{:S(2)}) copy-start(s32[2,1024]{1,0:T(2,128)} %param.16) | copy-start | bytes 24580
  25.4 1002.0 %reduce-scatter.2.cloned.1.call-start = ((), (), s32[]{:S(2)}) async-start(), calls=%async_computation.2 | async-start | bytes 294912 | tf_op jit(solution)/shard_map/reduce_scatter | solution.py:128
  128.0 2.6 collective-permute-start
  129.4 5.0 collective-permute-start.1
  452.6 10.6 %collective-permute-start.2 = (f32[6,256]{1,0:T(8,128)S(1)}, f32[6,256]{1,0:T(8,128)S(1)}, u32[]{:S(2)}, u32[]{:S(2)}) collective-permute-start(f32[6,256]{1,0:T(8,128)S(1)} %copy.158), channel_id=1, source_target_pairs={{0,8},{8,16},{16,24},{1,9},{9,17},{17,25},{2,10},{10,18},{18,26},{... | collective-permute-start | bytes 18440 | tf_op jit(solution)/shard_map/ppermute | solution.py:22
  461.9 106.6 %collective-permute-start.3 = (f32[6,256]{1,0:T(8,128)S(1)}, f32[6,256]{1,0:T(8,128)S(1)}, u32[]{:S(2)}, u32[]{:S(2)}) collective-permute-start(f32[6,256]{1,0:T(8,128)S(1)} %copy.159), channel_id=1, source_target_pairs={{8,0},{16,8},{24,16},{9,1},{17,9},{25,17},{10,2},{18,10},{26,18},{... | collective-permute-start | bytes 18440 | tf_op jit(solution)/shard_map/ppermute | solution.py:24
  568.5 0.7 copy-start
Sparse Core Ops, SparseCore 0:
  25.5 101.4 all-gather.1
  569.3 458.0 reduce-scatter.1
where the time goes:
time: 1040 us
  waiting for transfers between devices  667 us (64%)
  other arithmetic  194 us (19%)
  local copies, waits for them, and re-layouts  142 us (14%)
  between operations  14.8 us (1%)
  matrix products  11 us (1%)
    reduce_scatter x1, waiting for transfers between devices, shards(): summed = lax.psum_scatter(interior, 'dev', scatter_dimension=1, tiled=True)  458 us
    ppermute x2, waiting for transfers between devices, padded(): lax.ppermute(head, axis, [((i + 1) % count, i) for i in range(ends)])  108 us
    all_gather x1, waiting for transfers between devices, shards(): gathered = lax.all_gather(own_spheres, 'dev', axis=0, tiled=True)  101 us
    gather x24, local copies, waits for them, and re-layouts, visit_block(): near_pos = spheres[first_block]  49.7 us
    gather x24, local copies, waits for them, and re-layouts, visit_block(): far_pos = spheres[second_block]  49.7 us
    reduce_sum x12, other arithmetic, contact(): return (jnp.sum(pushes, 2), -jnp.sum(pushes, 1))  48.9 us
    scatter-add x12, other arithmetic, visit_block(): totals.at[first_block]  43.3 us
    scatter-add x12, other arithmetic, visit_block(): totals.at[second_block]  43.3 us
  transfers between devices with their start and end apart: 6, of which 4 were waited for; matrix products, arithmetic and copies ran while one was open for 1% of the time, Pallas kernels for 0%

commit v1 on v0

v1 whole, which is shorter than its diff:
```python
import functools

import jax
import jax.numpy as jnp
from jax import lax
from jax.experimental import pallas as pl
from jax.experimental.pallas import tpu as pltpu
from jax.sharding import PartitionSpec as P

RIM = 128
LANES = 128
OFFSET_UNIT = 0.125
REACH_SQUARED = 4.0
STIFFNESS = 1.0 / 256.0
CHUNK = 64
UNROLL = 4
FORM = 32
COMPS = 12


def cross_axis(left_vec, right_vec):
    return jnp.stack(
        [
            left_vec[1] * right_vec[2] - left_vec[2] * right_vec[1],
            left_vec[2] * right_vec[0] - left_vec[0] * right_vec[2],
            left_vec[0] * right_vec[1] - left_vec[1] * right_vec[0],
        ],
        0,
    )


def split3(value):
    high = value.astype(jnp.bfloat16).astype(jnp.float32)
    rest = value - high
    middle = rest.astype(jnp.bfloat16).astype(jnp.float32)
    return high, middle, rest - middle


def pair_kernel(
    members, slots, head_row,
    place_ref, *refs,
):
    piece_count = members // 2
    pieces = refs[:piece_count]
    (rim_ref, off_ref, inner_ref, edge_ref, table, lists, gathered, form_a, form_b, form_c,
     form_v, spots, acc, sems) = refs[piece_count:]
    along_z, along_y, group = place_ref[0], place_ref[1], place_ref[2]
    own_rows = pieces[0].shape[1] - head_row
    inner_blocks = members * own_rows * 4
    slot_rows = slots // LANES
    spots_of = LANES // 4

    copies = []
    owners = []
    for k in range(piece_count):
        for side in range(2):
            member = lax.rem(along_z - k + piece_count, piece_count) * 2 + (
                along_y if side == 0 else 1 - along_y
            )
            owners.append(member)
            copy = pltpu.make_async_copy(
                pieces[k].at[side, pl.ds(0, head_row + 8)], lists.at[member], sems.at[2 * k + side]
            )
            copy.start()
            copies.append(copy)

    def unpack(source, row, first):
        rows = source[pl.ds(row, 32), :]
        for sub in range(4):
            shifted = rows if sub == 0 else pltpu.roll(rows, LANES - 32 * sub, axis=1)
            table[pl.ds(pl.multiple_of(first + sub * 32, 32), 32), :] = shifted

    for k in range(piece_count):
        for side in range(2):
            base = owners[2 * k + side] * (own_rows * 4)

            def take(part, carry, k=k, side=side, base=base):
                unpack(
                    pieces[k].at[side],
                    pl.multiple_of(head_row + part * 32, 8),
                    base + part * LANES,
                )
                return carry

            lax.fori_loop(0, own_rows // 32, take, 0)
    for end in range(2):
        unpack(rim_ref, end * 32, inner_blocks + end * LANES)

    acc[...] = jnp.zeros_like(acc)
    form_a[...] = jnp.zeros_like(form_a)
    form_b[...] = jnp.zeros_like(form_b)
    form_c[...] = jnp.zeros_like(form_c)
    form_v[...] = jnp.zeros_like(form_v)
    ones = jnp.ones((CHUNK, LANES), jnp.float32)
    lane_wide = lax.broadcasted_iota(jnp.int32, (CHUNK, LANES), 1)
    low_half = (lane_wide < LANES // 2).astype(jnp.float32)
    high_half = 1.0 - low_half
    for row in range(3):
        form_a[pl.ds(21 + row, CHUNK, stride=FORM), :] = ones
        form_b[pl.ds(18 + row, CHUNK, stride=FORM), :] = ones
        form_c[pl.ds(24 + row, CHUNK, stride=FORM), :] = low_half
        form_c[pl.ds(28 + row, CHUNK, stride=FORM), :] = high_half

    for copy in copies:
        copy.wait()
    cumulative = [jnp.int32(0)]
    for member in range(members):
        count = lists[member, head_row, 15].astype(jnp.int32)
        cumulative.append(cumulative[-1] + count)
    total = cumulative[-1]
    me = along_z * 2 + along_y
    begin = (total * me) // members
    finish = (total * (me + 1)) // members

    group_base = group * inner_blocks
    lane = lax.broadcasted_iota(jnp.int32, (2 * CHUNK, LANES), 1)
    lane8 = lax.broadcasted_iota(jnp.int32, (24, LANES), 1)
    row_sum = lax.broadcasted_iota(jnp.int32, (3 * LANES, 2 * LANES), 0)
    col_sum = lax.broadcasted_iota(jnp.int32, (3 * LANES, 2 * LANES), 1)
    halves = (((row_sum & (LANES - 1)) >= LANES // 2) == (col_sum >= LANES)).astype(jnp.bfloat16)

    def local_block(value):
        block = value.astype(jnp.int32) - group_base
        block = jnp.where(
            block < 0,
            block + inner_blocks + LANES,
            jnp.where(block >= inner_blocks, block + LANES, block),
        )
        return block

    def table_row(block):
        return (block & ~(LANES - 1)) | ((block & 3) << 5) | ((block >> 2) & (spots_of - 1))

    def fetch(first):
        def step(turn, carry):
            for sub in range(4):
                index = turn * 4 + sub
                at = jnp.minimum(first + index, finish - 1)
                member = jnp.int32(0)
                before = jnp.int32(0)
                for other in range(1, members):
                    past = at >= cumulative[other]
                    member = member + past.astype(jnp.int32)
                    before = jnp.where(past, cumulative[other], before)
                slot = at - before
                near = local_block(lists[member, slot >> 7, slot & (LANES - 1)])
                far = local_block(lists[member, slot_rows + (slot >> 7), slot & (LANES - 1)])
                gathered[pl.ds(index, 1), :] = table[pl.ds(table_row(near), 1), :]
                gathered[pl.ds(CHUNK + index, 1), :] = table[pl.ds(table_row(far), 1), :]
                spots[0, index] = near
                spots[1, index] = far
            return carry

        lax.fori_loop(0, CHUNK // 4, step, 0)

    def arrange():
        packed = gathered[...]

        def both(column):
            even = jnp.broadcast_to(packed[:, column : column + 1], packed.shape)
            odd = jnp.broadcast_to(packed[:, 16 + column : 17 + column], packed.shape)
            return even, odd

        def spread(column):
            even, odd = both(column)
            return jnp.where(lane < LANES // 2, even, odd)

        kind_even, kind_odd = both(12)
        lane_f = lane.astype(jnp.float32)
        pick = jnp.where(
            ((lane < 8) & (kind_even == lane_f)) | ((lane >= 8) & (kind_odd == lane_f - 8.0)),
            1.0,
            0.0,
        ).astype(jnp.bfloat16)
        offsets = jnp.dot(pick, off_ref[...], preferred_element_type=jnp.float32)
        where_at = []
        for axis in range(3):
            value = spread(axis)
            for mode in range(3):
                value = value + spread(3 + 3 * axis + mode) * offsets[:, mode * LANES : (mode + 1) * LANES]
            where_at.append(value)
        near = [value[:CHUNK] for value in where_at]
        far = [value[CHUNK:] for value in where_at]
        near_sq = near[0] * near[0] + near[1] * near[1] + near[2] * near[2]
        far_sq = far[0] * far[0] + far[1] * far[1] + far[2] * far[2]

        def put(form, row, value):
            form[pl.ds(row, CHUNK, stride=FORM), :] = value

        for axis in range(3):
            parts = split3(near[axis])
            for place, part in enumerate((0, 0, 1, 1, 0, 2)):
                put(form_a, 3 * place + axis, parts[part] * 2.0)
            for part in range(3):
                put(form_c, 8 * part + axis, parts[part] * low_half)
                put(form_c, 8 * part + 4 + axis, parts[part] * high_half)
            parts = split3(far[axis])
            for place, part in enumerate((0, 1, 0, 1, 2, 0)):
                put(form_b, 3 * place + axis, parts[part])
            for turn in range(3):
                spot = (axis - turn + 3) % 3
                put(form_v, 8 * turn + spot, far[axis])
                put(form_v, 8 * turn + 4 + spot, far[axis])
        for part, value in enumerate(split3(REACH_SQUARED - near_sq)):
            put(form_a, 18 + part, value)
        for part, value in enumerate(split3(-far_sq)):
            put(form_b, 21 + part, value)

    def meet(index, first):
        at = pl.ds(pl.multiple_of(index * FORM, FORM), FORM)
        near = form_a[at, :].astype(jnp.bfloat16)
        far = form_b[at, :].astype(jnp.bfloat16)
        reach = lax.dot_general(
            near, far, (((0,), (0,)), ((), ())), preferred_element_type=jnp.float32
        )
        weight = jnp.maximum(reach, 0.0)
        weight_high = weight.astype(jnp.bfloat16)
        weight_low = (weight - weight_high.astype(jnp.float32)).astype(jnp.bfloat16)
        side = form_c[at, :].astype(jnp.bfloat16)
        sums = jnp.dot(
            jnp.concatenate([side, side], 1),
            jnp.concatenate([weight_high, weight_low], 0),
            preferred_element_type=jnp.float32,
        )
        spot = form_v[at, :]
        force = sums[24:32] * spot[0:8] - (sums[0:8] + sums[8:16] + sums[16:24])
        terms = jnp.concatenate([force, force * spot[8:16], force * spot[16:24]], 0)
        parts = split3(terms)
        joined = jnp.concatenate([part.astype(jnp.bfloat16) for part in parts], 1)
        folded = jnp.dot(joined, halves, preferred_element_type=jnp.float32)
        lower = folded[:, :LANES]
        upper = folded[:, LANES:]
        live = first + index < finish
        block = spots[0, index]
        own = jnp.where(live, block & (LANES - 1), -1)
        here = lane8 == own
        base = pl.multiple_of((block >> 7) * 72, 8)
        acc[pl.ds(base, 24), :] += jnp.where(here, lower + upper, 0.0)
        block = spots[1, index]
        own = jnp.where(live, block & (LANES - 1), -1)
        here = lane8 == own
        base = pl.multiple_of((block >> 7) * 72 + 24, 8)
        acc[pl.ds(base, 24), :] += jnp.where(here, lower, 0.0)
        base = pl.multiple_of((block >> 7) * 72 + 48, 8)
        acc[pl.ds(base, 24), :] += jnp.where(here, upper, 0.0)

    def chunk(turn, carry):
        first = begin + turn * CHUNK
        fetch(first)
        arrange()
        todo = jnp.minimum(finish - first, CHUNK)

        def step(turn, carry):
            for sub in range(UNROLL):
                meet(turn * UNROLL + sub, first)
            return carry

        lax.fori_loop(0, (todo + UNROLL - 1) // UNROLL, step, 0)
        return carry

    lax.fori_loop(0, (finish - begin + CHUNK - 1) // CHUNK, chunk, 0)

    def total_of(row, half, tiles, start):
        def get(which, line):
            return acc[pl.ds(start * 72 + which * 24 + line, tiles, stride=72), :]

        line = (row // 3) * 8 + row % 3
        mine = get(0, line + 4 * half)
        other = get(1 + half, line) + get(1 + half, line + 4)
        return (other - mine) * STIFFNESS

    for tiles, start, out in ((inner_blocks // LANES, 0, inner_ref), (2, inner_blocks // LANES, edge_ref)):
        for half in range(2):
            rows = [total_of(row, half, tiles, start) for row in range(9)]
            results = rows[0:3] + [rows[6 + (axis + 2) % 3] - rows[3 + (axis + 1) % 3] for axis in range(3)]
            for axis in range(6):
                out[pl.ds(6 * half + axis, tiles, stride=COMPS), :] = results[axis]


def neighbour_swap(rows_low, rows_high, axis):
    count = lax.axis_size(axis)
    index = lax.axis_index(axis)
    even = index % 2 == 0
    inside = [(i, i ^ 1) for i in range(count)]
    across = [(i, (i + 1) % count if i % 2 else (i - 1) % count) for i in range(count)]
    got_across = lax.ppermute(jnp.where(even, rows_low, rows_high), axis, across)
    got_inside = lax.ppermute(jnp.where(even, rows_high, rows_low), axis, inside)
    from_below = jnp.where(even, got_across, got_inside)
    from_above = jnp.where(even, got_inside, got_across)
    return from_below, from_above


def shards(positions, rotations, clump_kind, sub_offsets, pair_blocks, pair_count):
    members = lax.axis_size("dev")
    groups = lax.axis_size("grp")
    group = lax.axis_index("grp")
    me = lax.axis_index("dev")
    along_z, along_y = me // 2, me % 2
    rings = members // 2
    clumps = positions.shape[1]
    slots = pair_blocks.shape[1]
    own_blocks = clumps // 2
    kinds, _, subs = sub_offsets.shape
    head_row = 2 * slots // LANES

    values = jnp.concatenate(
        [
            positions,
            rotations,
            clump_kind.astype(jnp.float32)[None],
            jnp.zeros((3, clumps), jnp.float32),
        ],
        0,
    )
    values = values.T.reshape(own_blocks, 32)
    lane = lax.broadcasted_iota(jnp.int32, values.shape, 1)
    values = jnp.where(lane == 15, pair_count[0].astype(jnp.float32), values)
    packed = values.reshape(own_blocks // 4, LANES)
    payload = jnp.concatenate(
        [pair_blocks.astype(jnp.float32).reshape(head_row, LANES), packed], 0
    )

    pair_y = [(i, i ^ 1) for i in range(members)]
    both = jnp.stack([payload, lax.ppermute(payload, "dev", pair_y)])
    pieces = [both]
    for k in range(1, rings):
        pieces.append(
            lax.ppermute(both, "dev", [(i, (i + 2 * k) % members) for i in range(members)])
        )

    def piece_rows(member, start, count):
        z, y = member // 2, member % 2
        found = None
        for k in range(rings):
            rows = lax.dynamic_slice_in_dim(pieces[k], start, count, 1)
            side = jnp.where(along_y == y, rows[0], rows[1])
            hit = (along_z - k + rings) % rings == z
            found = side if found is None else jnp.where(hit, side, found)
        return found

    rim_rows = RIM // 4
    first_rows = piece_rows(0, head_row, rim_rows)
    last_rows = piece_rows(members - 1, head_row + packed.shape[0] - rim_rows, rim_rows)
    from_below, from_above = neighbour_swap(first_rows, last_rows, "grp")
    rims = jnp.concatenate([from_below, from_above], 0)

    offset_table = sub_offsets.astype(jnp.float32) * OFFSET_UNIT
    blank = jnp.zeros_like(offset_table)
    offset_rows = jnp.concatenate(
        [
            jnp.concatenate([offset_table, blank], 2).reshape(kinds, -1),
            jnp.concatenate([blank, offset_table], 2).reshape(kinds, -1),
        ],
        0,
    )
    offset_rows = jnp.concatenate(
        [offset_rows, jnp.zeros((LANES - 2 * kinds, offset_rows.shape[1]), jnp.float32)], 0
    ).astype(jnp.bfloat16)

    place = jnp.stack([along_z, along_y, group]).astype(jnp.int32)
    inner_blocks = own_blocks * members
    tiles = inner_blocks // LANES
    vmem = pl.BlockSpec(memory_space=pltpu.VMEM)
    inner, edge = pl.pallas_call(
        functools.partial(pair_kernel, members, slots, head_row),
        out_shape=(
            jax.ShapeDtypeStruct((tiles * COMPS, LANES), jnp.float32),
            jax.ShapeDtypeStruct((2 * COMPS, LANES), jnp.float32),
        ),
        in_specs=[pl.BlockSpec(memory_space=pltpu.SMEM)] + [vmem] * (rings + 2),
        out_specs=(vmem, vmem),
        scratch_shapes=[
            pltpu.VMEM((inner_blocks + 2 * RIM, LANES), jnp.float32),
            pltpu.SMEM((members, head_row + 8, LANES), jnp.float32),
            pltpu.VMEM((2 * CHUNK, LANES), jnp.float32),
            pltpu.VMEM((CHUNK * FORM, LANES), jnp.float32),
            pltpu.VMEM((CHUNK * FORM, LANES), jnp.float32),
            pltpu.VMEM((CHUNK * FORM, LANES), jnp.float32),
            pltpu.VMEM((CHUNK * FORM, LANES), jnp.float32),
            pltpu.SMEM((2, CHUNK), jnp.int32),
            pltpu.VMEM(((tiles + 2) * 72, LANES), jnp.float32),
            pltpu.SemaphoreType.DMA((members,)),
        ],
        name="pair_kernel",
    )(place, *pieces, rims, offset_rows)

    below, above = neighbour_swap(edge[:COMPS], edge[COMPS:], "grp")
    below = jnp.where(group > 0, below, 0.0)
    above = jnp.where(group < groups - 1, above, 0.0)
    inner = inner.at[:COMPS].add(below)
    inner = inner.at[(tiles - 1) * COMPS :].add(above)

    own_rows = tiles * COMPS // members
    ranks = inner.reshape(rings, 2, own_rows, LANES)
    mine = lax.dynamic_index_in_dim(ranks, along_y, 1, False)
    other = lax.dynamic_index_in_dim(ranks, 1 - along_y, 1, False)
    column = mine + lax.ppermute(other, "dev", pair_y)
    summed = lax.dynamic_index_in_dim(column, along_z, 0, False)
    for k in range(1, rings):
        part = lax.dynamic_index_in_dim(column, (along_z + k) % rings, 0, False)
        summed = summed + lax.ppermute(
            part, "dev", [(i, (i + 2 * k) % members) for i in range(members)]
        )
    summed = summed.reshape(own_blocks // LANES, 2, 6, LANES).transpose(2, 0, 3, 1).reshape(6, clumps)
    clump_force = summed[0:3]
    clump_torque = summed[3:6] - cross_axis(positions, clump_force)
    return (clump_force, clump_torque)


def solution(mesh):
    placed = (
        P(None, ("grp", "dev")),
        P(None, ("grp", "dev")),
        P(("grp", "dev")),
        P(),
        P(None, ("grp", "dev")),
        P(("grp", "dev")),
    )
    return jax.shard_map(
        shards,
        mesh=mesh,
        in_specs=placed,
        out_specs=(P(None, ("grp", "dev")), P(None, ("grp", "dev"))),
        check_vma=False,
    )
```

time: 1040 us -> 189 us (0.18)
  waiting for transfers between devices: 667 us -> 18.5 us
  other arithmetic: 194 us -> 6.47 us
  local copies, waits for them, and re-layouts: 142 us -> 8.16 us
  Pallas kernels: 0 us -> 109 us
  starting transfers between devices: 5.26 us -> 46.3 us
  between operations: 14.8 us -> 1.54 us
  matrix products: 11 us -> 0 us
    reduce_scatter x1 -> x0, waiting for transfers between devices: 458 us -> none  [shards(): summed = lax.psum_scatter(interior, 'dev', scatter_dimension=1, tiled=True)]
    pallas_call x0 -> x1, Pallas kernels: none -> 109 us  [shards(): pl.pallas_call(functools.partial(pair_kernel, members, slots, head_row),...]
    all_gather x1 -> x0, waiting for transfers between devices: 101 us -> none  [shards(): gathered = lax.all_gather(own_spheres, 'dev', axis=0, tiled=True)]
    gather x48 -> x0, local copies, waits for them, and re-layouts: 99.5 us -> none  [the longest x24 49.7 us: visit_block(): near_pos = spheres[first_block]]
    ppermute x4 -> x12, waiting for transfers between devices: 108 us -> 18.5 us  [the longest x3 6.48 us: shards(): lax.ppermute(both, 'dev', [(i, (i + 2 * k) % members) for i in range(memb...]
    scatter-add x26 -> x0, other arithmetic: 87.3 us -> none  [the longest x12 43.3 us: visit_block(): totals.at[first_block]]
    reduce_sum x72 -> x0, other arithmetic: 82.4 us -> none  [the longest x12 48.9 us: contact(): return (jnp.sum(pushes, 2), -jnp.sum(pushes, 1))]
    ppermute x4 -> x12, starting transfers between devices: 5.18 us -> 46.3 us  [the longest x2 26.5 us: neighbour_swap(): lax.ppermute(jnp.where(even, rows_low, rows_high), axis, across)]
  transfers between devices with their start and end apart: 6 -> 12, of which waited for: 4 -> 8; matrix products, arithmetic and copies ran while one was open for 1% -> 1% of each run, Pallas kernels for 0% -> 0%
where the time goes in v1:
time: 189 us; the launch traced here: 190 us
  Pallas kernels  109 us (58%)
  starting transfers between devices  46.3 us (24%)
  waiting for transfers between devices  18.5 us (10%)
  local copies, waits for them, and re-layouts  8.16 us (4%)
  other arithmetic  6.47 us (3%)
    pallas_call x1, Pallas kernels, shards(): pl.pallas_call(functools.partial(pair_kernel, members, slots, head_row),...  109 us
    ppermute x2, starting transfers between devices, neighbour_swap(): lax.ppermute(jnp.where(even, rows_low, rows_high), axis, across)  26.5 us
    ppermute x3, waiting for transfers between devices, shards(): lax.ppermute(both, 'dev', [(i, (i + 2 * k) % members) for i in range(memb...  6.48 us
    ppermute x3, starting transfers between devices, shards(): lax.ppermute(part, 'dev', [(i, (i + 2 * k) % members) for i in range(memb...  6.07 us
    ppermute x3, starting transfers between devices, shards(): lax.ppermute(both, 'dev', [(i, (i + 2 * k) % members) for i in range(memb...  6.07 us
    ppermute x3, waiting for transfers between devices, shards(): lax.ppermute(part, 'dev', [(i, (i + 2 * k) % members) for i in range(memb...  5.62 us
  transfers between devices with their start and end apart: 12, of which 8 were waited for; matrix products, arithmetic and copies ran while one was open for 1% of the time, Pallas kernels for 0%

profile of v1, /device:TPU:0, one launch (start us, length us, event | category | flops | bytes accessed | tf_op | source)
XLA Modules:
  0.0 190.4 jit_solution(14401855642371551923)
XLA Ops:
  0.6 0.7 convert_element_type.19
  1.3 0.1 pad.23.clone
  1.4 0.9 maximum_bitcast_fusion
  2.3 0.2 copy.9
  2.5 0.0 copy-start.7
  2.5 0.2 reshape.121
  2.7 0.1 iota.12
  3.5 0.0 copy-done.7
  3.6 3.1 %collective-permute-start = (f32[144,128]{1,0:T(8,128)S(1)}, f32[144,128]{1,0:T(8,128)S(1)}, u32[]{:S(2)}, u32[]{:S(2)}) collective-permute-start(f32[144,128]{1,0:T(8,128)S(1)} %get-tuple-element.37), channel_id=1, source_target_pairs={{0,1},{1,0},{2,3},{3,2},{4,5},{5,4},{6,7},{7,6},{8,9},{9,8},{10,11... | collective-permute-start | bytes 221192 | tf_op jit(solution)/shard_map/ppermute | solution.py:324
  6.6 0.7 copy-done.6
  7.3 0.1 pad.13.clone
  7.4 0.1 pad_bitcast_fusion.1
  7.5 1.5 collective-permute-done
  9.0 0.0 copy-start
  9.0 2.1 %collective-permute-start.1 = (f32[2,144,128]{2,1,0:T(8,128)S(1)}, f32[2,144,128]{2,1,0:T(8,128)S(1)}, u32[]{:S(2)}, u32[]{:S(2)}) collective-permute-start(f32[2,144,128]{2,1,0:T(8,128)S(1)} %pad_maximum_fusion.refs_0_), channel_id=1, source_target_pairs={{0,2},{1,3},{2,4},{3,5},{4,6},{5,7},{6,0},{7,1},{8,10},{9,11},{10,... | collective-permute-start | bytes 442376 | tf_op jit(solution)/shard_map/ppermute | solution.py:328
  11.1 2.6 %collective-permute-start.2 = (f32[2,144,128]{2,1,0:T(8,128)S(1)}, f32[2,144,128]{2,1,0:T(8,128)S(1)}, u32[]{:S(2)}, u32[]{:S(2)}) collective-permute-start(f32[2,144,128]{2,1,0:T(8,128)S(1)} %pad_maximum_fusion.refs_0_), channel_id=1, source_target_pairs={{0,4},{1,5},{2,6},{3,7},{4,0},{5,1},{6,2},{7,3},{8,12},{9,13},{10,... | collective-permute-start | bytes 442376 | tf_op jit(solution)/shard_map/ppermute | solution.py:328
  13.7 1.3 collective-permute-start.3
  15.1 0.7 maximum_maximum_fusion.refs_5_
  15.8 2.2 %collective-permute-done.1.refs_1_ = f32[2,144,128]{2,1,0:T(8,128)S(1)} collective-permute-done((f32[2,144,128]{2,1,0:T(8,128)S(1)}, f32[2,144,128]{2,1,0:T(8,128)S(1)}, u32[]{:S(2)}, u32[]{:S(2)}) %collective-permute-start.1) | collective-permute-done | bytes 147488 | tf_op jit(solution)/shard_map/ppermute | solution.py:328
  18.0 4.3 %collective-permute-done.2.refs_2_ = f32[2,144,128]{2,1,0:T(8,128)S(1)} collective-permute-done((f32[2,144,128]{2,1,0:T(8,128)S(1)}, f32[2,144,128]{2,1,0:T(8,128)S(1)}, u32[]{:S(2)}, u32[]{:S(2)}) %collective-permute-start.2) | collective-permute-done | bytes 147488 | tf_op jit(solution)/shard_map/ppermute | solution.py:328
  22.3 0.0 collective-permute-done.3.refs_3_
  22.3 0.0 copy-done
  22.3 0.0 copy-done.1
  22.3 0.1 collective-permute-start.5
  22.4 1.6 collective-permute-start.4
  24.0 0.6 pad_add_fusion.place_ref
  24.6 0.0 collective-permute-done.5
  24.6 1.0 collective-permute-done.4
  25.6 0.6 pad_maximum_fusion.2.refs_4_
  26.2 0.0 copy-done.2
  26.2 0.0 copy-done.3
  26.2 109.5 %pair_kernel.1 = (f32[384,128]{1,0:T(8,128)}, f32[24,128]{1,0:T(8,128)}) custom-call(s32[3]{0:T(128)} %pad_add_fusion.place_ref, f32[2,144,128]{2,1,0:T(8,128)} %copy-done, f32[2,144,128]{2,1,0:T(8,128)} %copy-done.1, f32[2,144,128]{2,1,0:T(8,128)} %copy-done.2, f32[2,144,128]{2,1,0:T(8,128)} %copy-done.3, f32[64,128]{1,0:T(8,128)} %pad_maximum_fusion.2.refs_4_, ...), custom_call_target="tpu_custom_call" | custom-call | tf_op jit(solution)/shard_map/pair_kernel/pallas_call | solution.py:364
  135.8 0.8 slice_select_fusion.8
  136.5 24.9 %collective-permute-start.6 = (f32[12,128]{1,0:T(8,128)S(1)}, f32[12,128]{1,0:T(8,128)S(1)}, u32[]{:S(2)}, u32[]{:S(2)}) collective-permute-start(f32[12,128]{1,0:T(8,128)S(1)} %get-tuple-element.49), channel_id=1, source_target_pairs={{0,24},{8,16},{16,8},{24,0},{1,25},{9,17},{17,9},{25,1},{2,26},{10... | collective-permute-start | bytes 18440 | tf_op jit(solution)/shard_map/ppermute | solution.py:286
  161.5 2.9 %collective-permute-start.7 = (f32[12,128]{1,0:T(8,128)S(1)}, f32[12,128]{1,0:T(8,128)S(1)}, u32[]{:S(2)}, u32[]{:S(2)}) collective-permute-start(f32[12,128]{1,0:T(8,128)S(1)} %get-tuple-element.48), channel_id=1, source_target_pairs={{0,8},{8,0},{16,24},{24,16},{1,9},{9,1},{17,25},{25,17},{2,10},{10... | collective-permute-start | bytes 18440 | tf_op jit(solution)/shard_map/ppermute | solution.py:287
  164.4 0.0 collective-permute-done.6
  164.4 0.8 collective-permute-done.7
  165.2 0.7 select_add_fusion
  165.9 1.3 scatter-add.6
  167.2 0.7 slice_add_fusion
  167.9 1.3 scatter-add.9
  169.2 1.0 dynamic-slice_bitcast_fusion
  170.2 1.5 collective-permute-start.8
  171.8 3.1 %collective-permute-done.8 = f32[4,48,128]{2,1,0:T(8,128)S(1)} collective-permute-done((f32[4,48,128]{2,1,0:T(8,128)S(1)}, f32[4,48,128]{2,1,0:T(8,128)S(1)}, u32[]{:S(2)}, u32[]{:S(2)}) %collective-permute-start.8) | collective-permute-done | bytes 98336 | tf_op jit(solution)/shard_map/ppermute | solution.py:397
  174.8 0.0 copy-done.4
  174.9 2.9 %collective-permute-start.10 = (f32[48,128]{1,0:T(8,128)S(1)}, f32[48,128]{1,0:T(8,128)S(1)}, u32[]{:S(2)}, u32[]{:S(2)}) collective-permute-start(f32[48,128]{1,0:T(8,128)S(1)} %get-tuple-element.35), channel_id=1, source_target_pairs={{0,4},{1,5},{2,6},{3,7},{4,0},{5,1},{6,2},{7,3},{8,12},{9,13},{10,... | collective-permute-start | bytes 73736 | tf_op jit(solution)/shard_map/ppermute | solution.py:401
  177.7 3.2 %collective-permute-start.11 = (f32[48,128]{1,0:T(8,128)S(1)}, f32[48,128]{1,0:T(8,128)S(1)}, u32[]{:S(2)}, u32[]{:S(2)}) collective-permute-start(f32[48,128]{1,0:T(8,128)S(1)} %get-tuple-element.34), channel_id=1, source_target_pairs={{0,6},{1,7},{2,0},{3,1},{4,2},{5,3},{6,4},{7,5},{8,14},{9,15},{10,... | collective-permute-start | bytes 73736 | tf_op jit(solution)/shard_map/ppermute | solution.py:401
  180.9 0.0 collective-permute-start.9
  180.9 0.0 collective-permute-done.10
  180.9 1.6 collective-permute-done.11
  182.5 4.0 %collective-permute-done.9 = f32[48,128]{1,0:T(8,128)S(1)} collective-permute-done((f32[48,128]{1,0:T(8,128)S(1)}, f32[48,128]{1,0:T(8,128)S(1)}, u32[]{:S(2)}, u32[]{:S(2)}) %collective-permute-start.9) | collective-permute-done | bytes 24608 | tf_op jit(solution)/shard_map/ppermute | solution.py:401
  186.6 0.1 copy.12
  186.8 0.2 squeeze.32
  187.0 0.1 copy.13
  187.1 0.2 squeeze.62
  187.3 0.1 copy.14
  187.5 0.2 squeeze.63
  187.6 0.3 copy.11
  187.9 0.5 slice.177
  188.4 0.3 copy.10
  188.7 0.0 copy-start.5
  188.7 1.1 slice.175
  189.8 0.0 copy-done.5
  189.8 0.6 maximum_subtract_fusion
  (25 shorter events, 0.2 us)
Async XLA Ops:
  2.5 1.0 copy-start.7
  3.6 5.4 %collective-permute-start = (f32[144,128]{1,0:T(8,128)S(1)}, f32[144,128]{1,0:T(8,128)S(1)}, u32[]{:S(2)}, u32[]{:S(2)}) collective-permute-start(f32[144,128]{1,0:T(8,128)S(1)} %get-tuple-element.37), channel_id=1, source_target_pairs={{0,1},{1,0},{2,3},{3,2},{4,5},{5,4},{6,7},{7,6},{8,9},{9,8},{10,11... | collective-permute-start | bytes 221192 | tf_op jit(solution)/shard_map/ppermute | solution.py:324
  6.6 0.7 copy-start.6
  9.0 13.3 %copy-start = (f32[2,144,128]{2,1,0:T(8,128)}, f32[2,144,128]{2,1,0:T(8,128)S(1)}, u32[]{:S(2)}) copy-start(f32[2,144,128]{2,1,0:T(8,128)S(1)} %pad_maximum_fusion.refs_0_) | copy-start | bytes 442372
  9.0 9.0 %collective-permute-start.1 = (f32[2,144,128]{2,1,0:T(8,128)S(1)}, f32[2,144,128]{2,1,0:T(8,128)S(1)}, u32[]{:S(2)}, u32[]{:S(2)}) collective-permute-start(f32[2,144,128]{2,1,0:T(8,128)S(1)} %pad_maximum_fusion.refs_0_), channel_id=1, source_target_pairs={{0,2},{1,3},{2,4},{3,5},{4,6},{5,7},{6,0},{7,1},{8,10},{9,11},{10,... | collective-permute-start | bytes 442376 | tf_op jit(solution)/shard_map/ppermute | solution.py:328
  11.1 11.1 %collective-permute-start.2 = (f32[2,144,128]{2,1,0:T(8,128)S(1)}, f32[2,144,128]{2,1,0:T(8,128)S(1)}, u32[]{:S(2)}, u32[]{:S(2)}) collective-permute-start(f32[2,144,128]{2,1,0:T(8,128)S(1)} %pad_maximum_fusion.refs_0_), channel_id=1, source_target_pairs={{0,4},{1,5},{2,6},{3,7},{4,0},{5,1},{6,2},{7,3},{8,12},{9,13},{10,... | collective-permute-start | bytes 442376 | tf_op jit(solution)/shard_map/ppermute | solution.py:328
  13.7 8.6 %collective-permute-start.3 = (f32[2,144,128]{2,1,0:T(8,128)S(1)}, f32[2,144,128]{2,1,0:T(8,128)S(1)}, u32[]{:S(2)}, u32[]{:S(2)}) collective-permute-start(f32[2,144,128]{2,1,0:T(8,128)S(1)} %pad_maximum_fusion.refs_0_), channel_id=1, source_target_pairs={{0,6},{1,7},{2,0},{3,1},{4,2},{5,3},{6,4},{7,5},{8,14},{9,15},{10,... | collective-permute-start | bytes 442376 | tf_op jit(solution)/shard_map/ppermute | solution.py:328
  18.0 4.3 %copy-start.1 = (f32[2,144,128]{2,1,0:T(8,128)}, f32[2,144,128]{2,1,0:T(8,128)S(1)}, u32[]{:S(2)}) copy-start(f32[2,144,128]{2,1,0:T(8,128)S(1)} %collective-permute-done.1.refs_1_) | copy-start | bytes 442372
  22.3 4.0 %copy-start.2 = (f32[2,144,128]{2,1,0:T(8,128)}, f32[2,144,128]{2,1,0:T(8,128)S(1)}, u32[]{:S(2)}) copy-start(f32[2,144,128]{2,1,0:T(8,128)S(1)} %collective-permute-done.2.refs_2_) | copy-start | bytes 442372
  22.3 4.0 %copy-start.3 = (f32[2,144,128]{2,1,0:T(8,128)}, f32[2,144,128]{2,1,0:T(8,128)S(1)}, u32[]{:S(2)}) copy-start(f32[2,144,128]{2,1,0:T(8,128)S(1)} %collective-permute-done.3.refs_3_) | copy-start | bytes 442372
  22.3 2.3 %collective-permute-start.5 = (f32[32,128]{1,0:T(8,128)S(1)}, f32[32,128]{1,0:T(8,128)S(1)}, u32[]{:S(2)}, u32[]{:S(2)}) collective-permute-start(f32[32,128]{1,0:T(8,128)S(1)} %select_bitcast_fusion), channel_id=1, source_target_pairs={{0,8},{8,0},{16,24},{24,16},{1,9},{9,1},{17,25},{25,17},{2,10},{10... | collective-permute-start | bytes 49160 | tf_op jit(solution)/shard_map/ppermute | solution.py:287
  22.4 3.2 %collective-permute-start.4 = (f32[32,128]{1,0:T(8,128)S(1)}, f32[32,128]{1,0:T(8,128)S(1)}, u32[]{:S(2)}, u32[]{:S(2)}) collective-permute-start(f32[32,128]{1,0:T(8,128)S(1)} %get-tuple-element.30), channel_id=1, source_target_pairs={{0,24},{8,16},{16,8},{24,0},{1,25},{9,17},{17,9},{25,1},{2,26},{10... | collective-permute-start | bytes 49160 | tf_op jit(solution)/shard_map/ppermute | solution.py:286
  136.5 27.9 %collective-permute-start.6 = (f32[12,128]{1,0:T(8,128)S(1)}, f32[12,128]{1,0:T(8,128)S(1)}, u32[]{:S(2)}, u32[]{:S(2)}) collective-permute-start(f32[12,128]{1,0:T(8,128)S(1)} %get-tuple-element.49), channel_id=1, source_target_pairs={{0,24},{8,16},{16,8},{24,0},{1,25},{9,17},{17,9},{25,1},{2,26},{10... | collective-permute-start | bytes 18440 | tf_op jit(solution)/shard_map/ppermute | solution.py:286
  161.5 3.8 %collective-permute-start.7 = (f32[12,128]{1,0:T(8,128)S(1)}, f32[12,128]{1,0:T(8,128)S(1)}, u32[]{:S(2)}, u32[]{:S(2)}) collective-permute-start(f32[12,128]{1,0:T(8,128)S(1)} %get-tuple-element.48), channel_id=1, source_target_pairs={{0,8},{8,0},{16,24},{24,16},{1,9},{9,1},{17,25},{25,17},{2,10},{10... | collective-permute-start | bytes 18440 | tf_op jit(solution)/shard_map/ppermute | solution.py:287
  169.2 5.6 %copy-start.4 = (f32[384,128]{1,0:T(8,128)S(1)}, f32[384,128]{1,0:T(8,128)}, u32[]{:S(2)}) copy-start(f32[384,128]{1,0:T(8,128)} %scatter-add.9) | copy-start | bytes 589828
  170.2 4.6 %collective-permute-start.8 = (f32[4,48,128]{2,1,0:T(8,128)S(1)}, f32[4,48,128]{2,1,0:T(8,128)S(1)}, u32[]{:S(2)}, u32[]{:S(2)}) collective-permute-start(f32[4,48,128]{2,1,0:T(8,128)S(1)} %dynamic-slice_bitcast_fusion), channel_id=1, source_target_pairs={{0,1},{1,0},{2,3},{3,2},{4,5},{5,4},{6,7},{7,6},{8,9},{9,8},{10,11... | collective-permute-start | bytes 294920 | tf_op jit(solution)/shard_map/ppermute | solution.py:397
  174.9 6.1 %collective-permute-start.10 = (f32[48,128]{1,0:T(8,128)S(1)}, f32[48,128]{1,0:T(8,128)S(1)}, u32[]{:S(2)}, u32[]{:S(2)}) collective-permute-start(f32[48,128]{1,0:T(8,128)S(1)} %get-tuple-element.35), channel_id=1, source_target_pairs={{0,4},{1,5},{2,6},{3,7},{4,0},{5,1},{6,2},{7,3},{8,12},{9,13},{10,... | collective-permute-start | bytes 73736 | tf_op jit(solution)/shard_map/ppermute | solution.py:401
  177.7 4.8 %collective-permute-start.11 = (f32[48,128]{1,0:T(8,128)S(1)}, f32[48,128]{1,0:T(8,128)S(1)}, u32[]{:S(2)}, u32[]{:S(2)}) collective-permute-start(f32[48,128]{1,0:T(8,128)S(1)} %get-tuple-element.34), channel_id=1, source_target_pairs={{0,6},{1,7},{2,0},{3,1},{4,2},{5,3},{6,4},{7,5},{8,14},{9,15},{10,... | collective-permute-start | bytes 73736 | tf_op jit(solution)/shard_map/ppermute | solution.py:401
  180.9 5.6 %collective-permute-start.9 = (f32[48,128]{1,0:T(8,128)S(1)}, f32[48,128]{1,0:T(8,128)S(1)}, u32[]{:S(2)}, u32[]{:S(2)}) collective-permute-start(f32[48,128]{1,0:T(8,128)S(1)} %get-tuple-element.33), channel_id=1, source_target_pairs={{0,2},{1,3},{2,4},{3,5},{4,6},{5,7},{6,0},{7,1},{8,10},{9,11},{10,... | collective-permute-start | bytes 73736 | tf_op jit(solution)/shard_map/ppermute | solution.py:401
  188.7 1.1 copy-start.5
